TPU v7x, 128 devices: a whole 4x4x4 slice. The times are simulated.
128 devices in a mesh: fsdp: 128 (over y, z, x, core).
Axes of the slice: x: 4, y: 4, z: 4, core: 2. Of those that a mesh axis runs over, the one named last changes fastest.
Arguments:
- hidden_in: bfloat16 [16384, 1024], P('fsdp'), may hold values from -24 to 24
- norm1_gain: bfloat16 [1024], P('fsdp'), may hold values from 0.099609375 to 1.8984375
- in_weight: bfloat16 [1024, 3072], P('fsdp'), may hold values from -0.1875 to 0.1875
- conv_weight: bfloat16 [1024, 3], P('fsdp'), may hold values from -3 to 3
- out_weight: bfloat16 [1024, 1024], P('fsdp'), may hold values from -0.1875 to 0.1875
- norm2_gain: bfloat16 [1024], P('fsdp'), may hold values from 0.099609375 to 1.8984375
- gate_weight: bfloat16 [1024, 4608], P('fsdp'), may hold values from -0.1875 to 0.1875
- up_weight: bfloat16 [1024, 4608], P('fsdp'), may hold values from -0.1875 to 0.1875
- down_weight: bfloat16 [4608, 1024], P('fsdp'), may hold values from -0.125 to 0.125
- segment_ids: int32 [16384], P('fsdp'), may hold values from 0 to 63, never falling along the last dimension, each value on 1 to 512 neighbouring positions
- cotangent: bfloat16 [16384, 1024], P('fsdp'), may hold values from -6 to 6
Outputs:
- block_out: bfloat16 [16384, 1024], P('fsdp')
- input_grad: float32 [16384, 1024], P('fsdp')
- norm1_gain_grad: float32 [1024], P('fsdp')
- in_weight_grad: float32 [1024, 3072], P('fsdp')
- conv_weight_grad: float32 [1024, 3], P('fsdp')
- out_weight_grad: float32 [1024, 1024], P('fsdp')
- norm2_gain_grad: float32 [1024], P('fsdp')
- gate_weight_grad: float32 [1024, 4608], P('fsdp')
- up_weight_grad: float32 [1024, 4608], P('fsdp')
- down_weight_grad: float32 [4608, 1024], P('fsdp')
Inputs may be any that keep to these rules, and one draw needn't show every extreme that they name: `segment_ids`: document numbers never fall along the tokens; each document covers 1 to 512 tokens, one exactly 512.
All inputs are finite; a program needn't handle non-finite values.
Results may differ from a plain program's by a relative error of at most 0.011.
Values may be sent and summed in bfloat16 or wider, within the bound.
A program may use at most 192 MiB of HBM per device.

v0:
```python
import jax
import jax.numpy as jnp
from jax import lax
from jax.sharding import PartitionSpec as P

CONV = 3
EPS = 1e-05
LANE = 256


def shifted(value, axis, by):
    size = lax.axis_size(axis)
    pairs = [(i, i + by) for i in range(size) if 0 <= i + by < size]
    return lax.ppermute(value, axis, pairs)


def rms_scale(values):
    return lax.rsqrt(jnp.mean(values * values, axis=-1, keepdims=True) + EPS)


def pad_cols(x):
    extra = -x.shape[1] % LANE
    return jnp.pad(x, ((0, 0), (0, extra))) if extra else x


def gather_packed(pieces):
    widths = [p.shape[1] for p in pieces]
    packed = jnp.concatenate(pieces, axis=1)
    full = lax.all_gather(packed, "fsdp", axis=0, tiled=True)
    out, at = ([], 0)
    for w in widths:
        out.append(full[:, at : at + w])
        at += w
    return out


def scatter_packed(pieces):
    widths = [p.shape[1] for p in pieces]
    packed = jnp.concatenate(pieces, axis=1)
    mine = lax.optimization_barrier(
        lax.psum_scatter(packed, "fsdp", scatter_dimension=0, tiled=True)
    )
    out, at = ([], 0)
    for w in widths:
        out.append(mine[:, at : at + w])
        at += w
    return out


def per_device(
    hidden_in,
    norm1_gain,
    in_weight,
    conv_weight,
    out_weight,
    norm2_gain,
    gate_weight,
    up_weight,
    down_weight,
    segment_ids,
    cotangent,
):
    rows = hidden_in.shape[0]
    width = hidden_in.shape[1]
    per = in_weight.shape[0]
    n = lax.axis_size("fsdp")
    down_rows = down_weight.shape[0]
    small = jnp.concatenate([norm1_gain[:, None], norm2_gain[:, None], conv_weight], axis=1)
    n_small = small.shape[1]
    w_in, w_out, small_full = gather_packed([in_weight, out_weight, pad_cols(small)])
    w_gate, w_up, w_down_packed = gather_packed(
        [gate_weight, up_weight, down_weight.reshape(per, -1)]
    )
    w_down = w_down_packed.reshape(n * down_rows, width)
    gain1 = small_full[:, 0]
    gain2 = small_full[:, 1]
    w_conv = small_full[:, 2 : 2 + CONV]
    xf = hidden_in.astype(jnp.float32)
    s1 = rms_scale(xf)
    h = (xf * s1 * gain1.astype(jnp.float32)).astype(jnp.bfloat16)
    proj = jnp.dot(h, w_in, preferred_element_type=jnp.float32)
    bgate = proj[:, :width]
    cgate = proj[:, width : 2 * width]
    xv = proj[:, 2 * width :]
    bx = (bgate * xv).astype(jnp.bfloat16)
    prev_rows, prev_ids = shifted(
        (bx[rows - 2 :], segment_ids[rows - 2 :].astype(jnp.bfloat16)), "fsdp", 1
    )
    ext_bx = jnp.concatenate([prev_rows, bx], axis=0).astype(jnp.float32)
    ext_ids = jnp.concatenate([prev_ids.astype(jnp.int32), segment_ids], axis=0)
    taps = w_conv.astype(jnp.float32)
    masks = [
        (ext_ids[2 - k : 2 - k + rows] == segment_ids).astype(jnp.float32)[:, None]
        for k in range(CONV)
    ]
    conv_out = jnp.zeros((rows, width), jnp.float32)
    for k in range(CONV):
        conv_out = conv_out + taps[:, k] * masks[k] * ext_bx[2 - k : 2 - k + rows]
    y = (cgate * conv_out).astype(jnp.bfloat16)
    resid = xf + jnp.dot(y, w_out, preferred_element_type=jnp.float32)
    s2 = rms_scale(resid)
    gain2f = gain2.astype(jnp.float32)
    h2 = (resid * s2 * gain2f).astype(jnp.bfloat16)
    a = jnp.dot(h2, w_gate, preferred_element_type=jnp.float32)
    b = jnp.dot(h2, w_up, preferred_element_type=jnp.float32)
    sig = jax.nn.sigmoid(a)
    act = a * sig
    z = (act * b).astype(jnp.bfloat16)
    block_out = (resid + jnp.dot(z, w_down, preferred_element_type=jnp.float32)).astype(
        jnp.bfloat16
    )
    dz = lax.dot_general(
        cotangent, w_down, (((1,), (1,)), ((), ())), preferred_element_type=jnp.float32
    )
    da = (dz * b * sig * (1.0 + a * (1.0 - sig))).astype(jnp.bfloat16)
    db = (dz * act).astype(jnp.bfloat16)
    g_down = lax.dot_general(
        z, cotangent, (((0,), (0,)), ((), ())), preferred_element_type=jnp.float32
    )
    g_gate = lax.dot_general(h2, da, (((0,), (0,)), ((), ())), preferred_element_type=jnp.float32)
    g_up = lax.dot_general(h2, db, (((0,), (0,)), ((), ())), preferred_element_type=jnp.float32)
    own_gate, own_up, own_down = scatter_packed([g_gate, g_up, g_down.reshape(n * per, -1)])
    dh2 = lax.dot_general(da, w_gate, (((1,), (1,)), ((), ())), preferred_element_type=jnp.float32)
    dh2 = dh2 + lax.dot_general(
        db, w_up, (((1,), (1,)), ((), ())), preferred_element_type=jnp.float32
    )
    g_gain2 = jnp.sum(dh2 * resid * s2, axis=0)
    dn2 = dh2 * gain2f
    d_resid = (
        cotangent.astype(jnp.float32)
        + s2 * dn2
        - resid * (s2 * s2 * s2) * jnp.mean(dn2 * resid, axis=-1, keepdims=True)
    )
    d_out = d_resid.astype(jnp.bfloat16)
    g_out = lax.dot_general(y, d_out, (((0,), (0,)), ((), ())), preferred_element_type=jnp.float32)
    dy = lax.dot_general(d_out, w_out, (((1,), (1,)), ((), ())), preferred_element_type=jnp.float32)
    d_cgate = dy * conv_out
    d_conv = dy * cgate
    d_ext = jnp.zeros((rows + 2, width), jnp.float32)
    tap_cols = []
    for k in range(CONV):
        term = d_conv * masks[k]
        d_ext = d_ext + jnp.pad(taps[:, k] * term, ((2 - k, k), (0, 0)))
        tap_cols.append(jnp.sum(term * ext_bx[2 - k : 2 - k + rows], axis=0))
    g_conv = jnp.stack(tap_cols, axis=1)
    returned = shifted(d_ext[:2], "fsdp", -1)
    d_bx = d_ext[2:] + jnp.pad(returned, ((rows - 2, 0), (0, 0)))
    d_proj = jnp.concatenate([d_bx * xv, d_cgate, d_bx * bgate], axis=1).astype(jnp.bfloat16)
    g_in = lax.dot_general(h, d_proj, (((0,), (0,)), ((), ())), preferred_element_type=jnp.float32)
    dh = lax.dot_general(d_proj, w_in, (((1,), (1,)), ((), ())), preferred_element_type=jnp.float32)
    g_gain1 = jnp.sum(dh * xf * s1, axis=0)
    dn1 = dh * gain1.astype(jnp.float32)
    input_grad = (
        d_resid + s1 * dn1 - xf * (s1 * s1 * s1) * jnp.mean(dn1 * xf, axis=-1, keepdims=True)
    )
    g_small = jnp.concatenate([g_gain1[:, None], g_gain2[:, None], g_conv], axis=1)
    own_in, own_out, own_small = scatter_packed([g_in, g_out, pad_cols(g_small)])
    return (
        block_out,
        input_grad,
        own_small[:, 0],
        own_in,
        own_small[:, 2 : 2 + CONV],
        own_out,
        own_small[:, 1],
        own_gate,
        own_up,
        own_down.reshape(down_rows, width),
    )


def solution(mesh):
    return jax.shard_map(
        per_device,
        mesh=mesh,
        in_specs=(
            P("fsdp", None),
            P("fsdp"),
            P("fsdp", None),
            P("fsdp", None),
            P("fsdp", None),
            P("fsdp"),
            P("fsdp", None),
            P("fsdp", None),
            P("fsdp", None),
            P("fsdp"),
            P("fsdp", None),
        ),
        out_specs=(
            P("fsdp", None),
            P("fsdp", None),
            P("fsdp"),
            P("fsdp", None),
            P("fsdp", None),
            P("fsdp", None),
            P("fsdp"),
            P("fsdp", None),
            P("fsdp", None),
            P("fsdp", None),
        ),
        check_vma=False,
    )
```

profile of v0, /device:TPU:0, one launch (start us, length us, event | category | flops | bytes accessed | tf_op | source)
XLA Modules:
  0.0 1274.9 jit_solution(17129408030517518262)
XLA Ops:
  17.4 67.1 %all-gather.3.cloned.1.call-done = bf16[1024,4352]{1,0:T(8,128)(2,1)} async-done(((bf16[8,4352]{1,0:T(8,128)(2,1)}), bf16[1024,4352]{1,0:T(8,128)(2,1)}) %all-gather.3.cloned.1.call-update) | async-done | bytes 8912912 | tf_op jit(solution)/shard_map/all_gather | solution.py:29
  85.9 4.0 fusion.10
  89.9 2.2 collective-permute-start
  95.2 2.3 multiply_reduce_fusion.5
  97.6 85.5 %all-gather.5.cloned.1.call-done = bf16[1024,13824]{1,0:T(8,128)(2,1)} async-done(((bf16[8,13824]{1,0:T(8,128)(2,1)}), bf16[1024,13824]{1,0:T(8,128)(2,1)}) %all-gather.5.cloned.1.call-update) | async-done | bytes 28311568 | tf_op jit(solution)/shard_map/all_gather | solution.py:29
  183.1 7.9 slice.156
  191.1 17.4 %reshape.88 = bf16[4608,1024]{1,0:T(8,128)(2,1)} reshape(bf16[1024,4608]{1,0:T(8,128)(2,1)} %slice.156) | data formatting | bytes 18874368 | tf_op jit(solution)/shard_map/reshape | solution.py:74
  208.5 6.9 convolution_bitcast_fusion
  215.4 5.1 fusion.2
  220.5 5.8 multiply_convert_fusion.1
  226.3 7.6 fusion
  234.0 6.0 multiply_reduce_fusion.3
  240.3 2.7 fusion.34
  247.8 6.5 fusion.32
  254.2 3.0 fusion.31
  257.5 11.7 select_maximum_fusion
  269.2 7.9 fusion.45
  277.2 21.6 %reshape.89 = f32[1024,4608]{1,0:T(8,128)} reshape(f32[4608,1024]{1,0:T(8,128)} %fusion.45) | data formatting | bytes 37748736 | tf_op jit(solution)/shard_map/reshape | solution.py:122
  298.8 9.3 fusion.43
  308.1 7.9 fusion.44
  316.0 37.7 %pad_maximum_fusion = f32[1024,13824]{1,0:T(8,128)} fusion(f32[1024,4608]{1,0:T(8,128)} %reshape.89, f32[1024,4608]{1,0:T(8,128)} %fusion.44, f32[1024,4608]{1,0:T(8,128)} %fusion.43), kind=kLoop, calls=%fused_computation | loop fusion | flops 28311552 | bytes 113246208 | tf_op jit(solution)/shard_map/concatenate | solution.py:39
  353.7 5.9 fusion.23
  360.7 582.3 %reduce-scatter.3.cloned.1.call-done = f32[8,4352]{1,0:T(8,128)} async-done(((f32[1024,4352]{1,0:T(8,128)}), f32[8,4352]{1,0:T(8,128)}) %reduce-scatter.3.cloned.1.call-update) | async-done | bytes 139280 | tf_op jit(solution)/shard_map/reduce_scatter | solution.py:41
  948.7 317.1 %reduce-scatter.5.cloned.1.call-done = f32[8,13824]{1,0:T(8,128)} async-done(((f32[1024,13824]{1,0:T(8,128)}), f32[8,13824]{1,0:T(8,128)}) %reduce-scatter.5.cloned.1.call-update) | async-done | bytes 442384 | tf_op jit(solution)/shard_map/reduce_scatter | solution.py:41
  (88 shorter events, 29.3 us)
Async XLA Ops:
  7.2 77.3 %all-gather.3.cloned.1.call-start = ((), (), s32[]{:S(2)}) async-start(), calls=%async_computation.2 | async-start | bytes 8982528 | tf_op jit(solution)/shard_map/all_gather | solution.py:29
  9.5 173.6 %all-gather.5.cloned.1.call-start = ((), (), s32[]{:S(2)}) async-start(), calls=%async_computation.3 | async-start | bytes 28532736 | tf_op jit(solution)/shard_map/all_gather | solution.py:29
  12.2 930.7 %reduce-scatter.3.cloned.1.call-start = ((), (), s32[]{:S(2)}) async-start(), calls=%async_computation.4 | async-start | bytes 17965056 | tf_op jit(solution)/shard_map/reduce_scatter | solution.py:41
  13.0 2.9 collective-permute-start.1
  85.9 9.3 copy-start.3
  89.9 4.2 copy-start
  89.9 4.0 collective-permute-start
  95.2 95.9 %copy-start.10 = (bf16[128,1024]{1,0:T(8,128)(2,1)}, bf16[128,1024]{1,0:T(8,128)(2,1)S(1)}, u32[]{:S(2)}) copy-start(bf16[128,1024]{1,0:T(8,128)(2,1)S(1)} %get-tuple-element.55) | copy-start | bytes 786436
  191.1 17.4 %copy-start.2 = (bf16[128,1024]{1,0:T(8,128)(2,1)S(1)}, bf16[128,1024]{1,0:T(8,128)(2,1)}, u32[]{:S(2)}) copy-start(bf16[128,1024]{1,0:T(8,128)(2,1)} %param.21) | copy-start | bytes 786436
  226.3 7.6 copy-start.7
  226.3 7.7 copy-start.9
  233.9 9.1 slice-start
  234.0 6.3 copy-start.11
  234.0 9.0 slice-start.1
  234.0 9.0 slice-start.2
  240.1 3.8 copy-start.1
  240.1 3.8 copy-start.6
  243.8 3.9 copy-start.4
  244.4 3.2 collective-permute-start.2
  269.2 996.6 %reduce-scatter.5.cloned.1.call-start = ((), (), s32[]{:S(2)}) async-start(), calls=%async_computation.5 | async-start | bytes 57065472 | tf_op jit(solution)/shard_map/reduce_scatter | solution.py:41
  298.8 9.3 copy-start.8
  353.7 6.0 copy-start.5
  353.7 5.9 copy-start.12
  353.7 5.9 copy-start.13
Sparse Core Ops, SparseCore 0:
  11.5 72.8 all-gather.2
  87.5 95.5 all-gather.4
  269.3 673.5 reduce-scatter.2
  949.2 316.6 reduce-scatter.4
where the time goes:
time: 1280 us; the launch traced here: 1270 us
  waiting for transfers between devices  1050 us (82%)
  matrix products  81.7 us (6%)
  other arithmetic  62.7 us (5%)
  local copies, waits for them, and re-layouts  57.6 us (4%)
  between operations  14.2 us (1%)
    reduce_scatter x2, waiting for transfers between devices, scatter_packed(): lax.psum_scatter(packed, 'fsdp', scatter_dimension=0, tiled=True)  899 us
    all_gather x2, waiting for transfers between devices, gather_packed(): full = lax.all_gather(packed, 'fsdp', axis=0, tiled=True)  153 us
    concatenate x2, other arithmetic, scatter_packed(): packed = jnp.concatenate(pieces, axis=1)  49.4 us
  transfers between devices with their start and end apart: 7, of which 5 were waited for; matrix products, arithmetic and copies ran while one was open for 9% of the time, Pallas kernels for 0%

commit v1 on v0

--- a/solution.py
+++ b/solution.py
@@ -26,7 +26,9 @@
 def gather_packed(pieces):
     widths = [p.shape[1] for p in pieces]
     packed = jnp.concatenate(pieces, axis=1)
-    full = lax.all_gather(packed, "fsdp", axis=0, tiled=True)
+    full = jnp.concatenate(
+        lax.all_to_all(jnp.stack([packed] * lax.axis_size("fsdp")), "fsdp", 0, 0), axis=0
+    )
     out, at = ([], 0)
     for w in widths:
         out.append(full[:, at : at + w])

time: 1280 us -> 1700 us (1.33)
  starting transfers between devices: 5.07 us -> 449 us
  waiting for transfers between devices: 1050 us -> 1020 us
    ppermute x3, starting transfers between devices: 4.91 us -> 422 us  [shifted(): return lax.ppermute(value, axis, pairs)]
    all_gather x2 -> x0, waiting for transfers between devices: 153 us -> none  [gather_packed(): full = lax.all_gather(packed, 'fsdp', axis=0, tiled=True)]
    all_to_all x0 -> x2, waiting for transfers between devices: none -> 106 us  [gather_packed(): lax.all_to_all(jnp.stack([packed] * lax.axis_size('fsdp')), 'fsdp', 0, 0)]
    all_to_all x0 -> x2, starting transfers between devices: none -> 27 us  [gather_packed(): lax.all_to_all(jnp.stack([packed] * lax.axis_size('fsdp')), 'fsdp', 0, 0)]
  transfers between devices with their start and end apart: 7 -> 7, of which waited for: 5 -> 5; matrix products, arithmetic and copies ran while one was open for 9% -> 6% of each run, Pallas kernels for 0% -> 0%
where the time goes in v1:
time: 1700 us
  waiting for transfers between devices  1020 us (60%)
  starting transfers between devices  449 us (26%)
  matrix products  87.4 us (5%)
  local copies, waits for them, and re-layouts  70.2 us (4%)
  other arithmetic  57.5 us (3%)
    reduce_scatter x2, waiting for transfers between devices, scatter_packed(): lax.psum_scatter(packed, 'fsdp', scatter_dimension=0, tiled=True)  909 us
    ppermute x3, starting transfers between devices, shifted(): return lax.ppermute(value, axis, pairs)  422 us
    all_to_all x2, waiting for transfers between devices, gather_packed(): lax.all_to_all(jnp.stack([packed] * lax.axis_size('fsdp')), 'fsdp', 0, 0)  106 us
    concatenate x2, other arithmetic, scatter_packed(): packed = jnp.concatenate(pieces, axis=1)  49.4 us
  transfers between devices with their start and end apart: 7, of which 5 were waited for; matrix products, arithmetic and copies ran while one was open for 6% of the time, Pallas kernels for 0%

profile of v1, /device:TPU:0, one launch (start us, length us, event | category | flops | bytes accessed | tf_op | source)
XLA Modules:
  0.0 1696.6 jit_solution(17517105492101904245)
XLA Ops:
  8.8 4.0 stack.10
  12.8 11.6 all-to-all-start
  24.6 106.2 %all-to-all-done = bf16[128,8,4352]{2,1,0:T(8,128)(2,1)} async-done(((bf16[128,8,4352]{2,1,0:T(8,128)(2,1)}), bf16[128,8,4352]{2,1,0:T(8,128)(2,1)}, u32[]{:S(2)}, u32[]{:S(2)}) %all-to-all-start) | async-done | bytes 8912928 | tf_op jit(solution)/shard_map/all_to_all | solution.py:30
  130.8 9.5 stack.11
  140.4 15.4 all-to-all-start.1
  163.4 418.8 %collective-permute-start = (bf16[2,1024]{1,0:T(2,128)(2,1)S(1)}, bf16[2,1024]{1,0:T(2,128)(2,1)S(1)}, u32[]{:S(2)}, u32[]{:S(2)}) collective-permute-start(bf16[2,1024]{1,0:T(2,128)(2,1)S(1)} %slice.146), channel_id=1, source_target_pairs={{0,1},{1,2},{2,3},{3,4},{4,5},{5,6},{6,7},{7,8},{8,9},{9,10},{10,1... | collective-permute-start | bytes 12296 | tf_op jit(solution)/shard_map/ppermute | solution.py:14
  587.6 7.9 slice.156
  595.6 6.5 fusion.2
  602.0 17.4 %reshape.100 = bf16[4608,1024]{1,0:T(8,128)(2,1)} reshape(bf16[1024,4608]{1,0:T(8,128)(2,1)} %slice.156) | data formatting | bytes 18874368 | tf_op jit(solution)/shard_map/reshape | solution.py:76
  619.5 7.0 convolution_bitcast_fusion
  626.5 5.8 multiply_convert_fusion.1
  632.4 7.6 fusion
  640.0 5.9 multiply_reduce_fusion.3
  657.0 5.9 fusion.31
  662.9 6.5 fusion.32
  669.7 11.7 select_maximum_fusion
  681.4 7.9 fusion.45
  689.3 21.6 %reshape.101 = f32[1024,4608]{1,0:T(8,128)} reshape(f32[4608,1024]{1,0:T(8,128)} %fusion.45) | data formatting | bytes 37748736 | tf_op jit(solution)/shard_map/reshape | solution.py:124
  710.9 9.3 fusion.43
  720.2 7.9 fusion.44
  728.1 37.7 %pad_maximum_fusion = f32[1024,13824]{1,0:T(8,128)} fusion(f32[1024,4608]{1,0:T(8,128)} %reshape.101, f32[1024,4608]{1,0:T(8,128)} %fusion.44, f32[1024,4608]{1,0:T(8,128)} %fusion.43), kind=kLoop, calls=%fused_computation | loop fusion | flops 28311552 | bytes 113246208 | tf_op jit(solution)/shard_map/concatenate | solution.py:41
  765.8 5.9 fusion.23
  772.7 591.5 %reduce-scatter.3.cloned.1.call-done = f32[8,4352]{1,0:T(8,128)} async-done(((f32[1024,4352]{1,0:T(8,128)}), f32[8,4352]{1,0:T(8,128)}) %reduce-scatter.3.cloned.1.call-update) | async-done | bytes 139280 | tf_op jit(solution)/shard_map/reduce_scatter | solution.py:43
  1370.0 317.2 %reduce-scatter.5.cloned.1.call-done = f32[8,13824]{1,0:T(8,128)} async-done(((f32[1024,13824]{1,0:T(8,128)}), f32[8,13824]{1,0:T(8,128)}) %reduce-scatter.5.cloned.1.call-update) | async-done | bytes 442384 | tf_op jit(solution)/shard_map/reduce_scatter | solution.py:43
  (91 shorter events, 35.4 us)
Async XLA Ops:
  12.8 11.6 copy-start.13
  12.8 11.7 copy-start.14
  12.8 11.8 copy-start.15
  12.8 118.0 %all-to-all-start = ((bf16[128,8,4352]{2,1,0:T(8,128)(2,1)}), bf16[128,8,4352]{2,1,0:T(8,128)(2,1)}, u32[]{:S(2)}, u32[]{:S(2)}) async-start(bf16[128,8,4352]{2,1,0:T(8,128)(2,1)} %stack.10), calls=%async_computation | async-start | bytes 17825792 | tf_op jit(solution)/shard_map/all_to_all | solution.py:30
  140.4 15.4 copy-start.16
  140.4 16.8 copy-start.3
  140.4 447.2 %all-to-all-start.1 = ((bf16[128,8,13824]{2,1,0:T(8,128)(2,1)}), bf16[128,8,13824]{2,1,0:T(8,128)(2,1)}, u32[]{:S(2)}, u32[]{:S(2)}) async-start(bf16[128,8,13824]{2,1,0:T(8,128)(2,1)} %stack.11), calls=%async_computation.1 | async-start | bytes 56623104 | tf_op jit(solution)/shard_map/all_to_all | solution.py:30
  155.7 1208.5 %reduce-scatter.3.cloned.1.call-start = ((), (), s32[]{:S(2)}) async-start(), calls=%async_computation.4 | async-start | bytes 17965056 | tf_op jit(solution)/shard_map/reduce_scatter | solution.py:43
  155.9 2.1 collective-permute-start.1
  163.3 420.8 %copy-start = (f32[128,3072]{1,0:T(8,128)}, f32[128,3072]{1,0:T(8,128)S(1)}, u32[]{:S(2)}) copy-start(f32[128,3072]{1,0:T(8,128)S(1)} %fusion.10) | copy-start | bytes 4718596
  163.4 420.6 %collective-permute-start = (bf16[2,1024]{1,0:T(2,128)(2,1)S(1)}, bf16[2,1024]{1,0:T(2,128)(2,1)S(1)}, u32[]{:S(2)}, u32[]{:S(2)}) collective-permute-start(bf16[2,1024]{1,0:T(2,128)(2,1)S(1)} %slice.146), channel_id=1, source_target_pairs={{0,1},{1,2},{2,3},{3,4},{4,5},{5,6},{6,7},{7,8},{8,9},{9,10},{10,1... | collective-permute-start | bytes 12296 | tf_op jit(solution)/shard_map/ppermute | solution.py:14
  585.2 10.3 copy-start.10
  602.0 17.4 %copy-start.2 = (bf16[128,1024]{1,0:T(8,128)(2,1)S(1)}, bf16[128,1024]{1,0:T(8,128)(2,1)}, u32[]{:S(2)}) copy-start(bf16[128,1024]{1,0:T(8,128)(2,1)} %param.21) | copy-start | bytes 786436
  619.5 7.0 copy-start.18
  632.4 7.6 copy-start.7
  632.4 7.6 copy-start.9
  640.0 8.7 copy-start.11
  651.5 5.6 copy-start.4
  651.9 4.9 collective-permute-start.2
  681.4 1005.9 %reduce-scatter.5.cloned.1.call-start = ((), (), s32[]{:S(2)}) async-start(), calls=%async_computation.5 | async-start | bytes 57065472 | tf_op jit(solution)/shard_map/reduce_scatter | solution.py:43
  710.9 9.3 copy-start.8
  765.8 5.9 copy-start.5
  765.8 5.9 copy-start.12
  765.8 5.9 copy-start.17
  (2 other events, 11.0 us)
Sparse Core Ops, SparseCore 0:
  681.5 682.6 reduce-scatter.2
  1370.6 316.5 reduce-scatter.4
